TPU v7x, 1024 devices: a whole 4x8x16 slice. The times are simulated.
1024 devices in a mesh: lat: 32 (over y_hi, z), lon: 32 (over y_lo, x, core).
Axes of the slice: x: 4, y: 8 (y_hi: 2, y_lo: 4; y = y_hi * 4 + y_lo), z: 16, core: 2. Of those that a mesh axis runs over, the one named last changes fastest.
Arguments:
- query_field: bfloat16 [256, 512, 768], P('lat', 'lon'), may hold values from -6 to 6
- key_field: bfloat16 [256, 512, 768], P('lat', 'lon'), may hold values from -6 to 6
- value_field: bfloat16 [256, 512, 768], P('lat', 'lon'), may hold values from -12 to 12
- out_cotangent: bfloat16 [256, 512, 768], P('lat', 'lon'), may hold values from -16 to 16
Outputs:
- attended: bfloat16 [256, 512, 768], P('lat', 'lon')
- query_grad: bfloat16 [256, 512, 768], P('lat', 'lon')
- key_grad: bfloat16 [256, 512, 768], P('lat', 'lon')
- value_grad: bfloat16 [256, 512, 768], P('lat', 'lon')
All inputs are finite; a program needn't handle non-finite values.
Results may differ from a plain program's by a relative error of at most 0.025.
Values may be sent and summed in bfloat16 or wider, within the bound.
No kernel may reach another device: no remote copies, remote signals or barrier semaphores. Data moves between devices by JAX's collectives and lax.ppermute only.
A program may use at most 128 MiB of HBM per device.

v0:
```python
import jax
import jax.numpy as jnp
from jax import lax
from jax.sharding import PartitionSpec as P

HEADS = 12
HEAD_DIM = 64
TILE = 8


def with_halo(cells, sides, width):
    for axis, dim in sides:
        count = lax.axis_size(axis)
        head = lax.slice_in_dim(cells, 0, width, axis=dim)
        tail = lax.slice_in_dim(cells, cells.shape[dim] - width, cells.shape[dim], axis=dim)
        cells = jnp.concatenate(
            [
                lax.ppermute(tail, axis, [(i, (i + 1) % count) for i in range(count)]),
                cells,
                lax.ppermute(head, axis, [((i + 1) % count, i) for i in range(count)]),
            ],
            axis=dim,
        )
    return cells


def from_behind(value, axis, by):
    size = lax.axis_size(axis)
    return lax.ppermute(value, axis, [(i, (i + by) % size) for i in range(size)])


def shifted(value, axis, steps):
    count = lax.axis_size(axis)
    initial, last = (max(0, -steps), min(count, count - steps))
    return lax.ppermute(value, axis, [(source, source + steps) for source in range(initial, last)])


def to_tiles(grid, head_count):
    grid_rows, grid_cols, features = grid.shape
    shaped = grid.reshape(
        grid_rows // TILE, TILE, grid_cols // TILE, TILE, head_count, features // head_count
    )
    return shaped.transpose(0, 2, 1, 3, 4, 5).reshape(
        grid_rows // TILE, grid_cols // TILE, TILE * TILE, head_count, features // head_count
    )


def from_tiles(tiles):
    tile_rows, tile_cols, cells, head_count, features = tiles.shape
    shaped = tiles.reshape(tile_rows, tile_cols, TILE, TILE, head_count * features)
    return shaped.transpose(0, 2, 1, 3, 4).reshape(
        tile_rows * TILE, tile_cols * TILE, head_count * features
    )


def gather_near(near, tile_rows, tile_cols, offsets, axis):
    pieces = [
        near[step_lat : step_lat + tile_rows, step_lon : step_lon + tile_cols]
        for step_lat, step_lon in offsets
    ]
    return jnp.concatenate(pieces, axis=axis)


def shards(query_field, key_field, value_field, out_cotangent):
    block_rows, block_cols = (query_field.shape[0], query_field.shape[1])
    tile_rows, tile_cols = (block_rows // TILE, block_cols // TILE)
    cells = TILE * TILE
    scaling = HEAD_DIM ** (-0.5)
    joined = jnp.concatenate([key_field, value_field], axis=-1)
    rimmed = with_halo(joined, (("lat", 0), ("lon", 1)), TILE)
    nearby = to_tiles(rimmed, 2 * HEADS)
    query_tiles = to_tiles(query_field, HEADS)
    grad_tiles = to_tiles(out_cotangent, HEADS)
    first_band = lax.axis_index("lat") * tile_rows
    band_count = tile_rows * lax.axis_size("lat")
    band_index = jnp.arange(tile_rows, dtype=jnp.int32)
    offsets = [(step_lat, step_lon) for step_lat in range(3) for step_lon in range(3)]

    def inside(step_lat):
        band = first_band + band_index + step_lat - 1
        return (band >= 0) & (band < band_count)

    valid_parts = [
        jnp.broadcast_to(inside(step_lat)[:, None], (tile_rows, cells))
        for step_lat, step_lon in offsets
    ]
    near_valid = jnp.concatenate(valid_parts, axis=1).reshape(tile_rows, 1, 1, 1, 9 * cells)
    near_all = gather_near(nearby, tile_rows, tile_cols, offsets, 2)
    keys_cat = near_all[:, :, :, :HEADS]
    values_cat = near_all[:, :, :, HEADS:]
    scores = (
        jnp.einsum("abqhd,abkhd->abhqk", query_tiles, keys_cat, preferred_element_type=jnp.float32)
        * scaling
    )
    scores = jnp.where(near_valid, scores, -jnp.inf)
    peak = jnp.max(scores, axis=-1, keepdims=True)
    log_total = peak + jnp.log(jnp.sum(jnp.exp(scores - peak), axis=-1, keepdims=True))
    weights = jnp.exp(scores - log_total)
    rounded = weights.astype(jnp.bfloat16)
    blended = jnp.einsum(
        "abhqk,abkhd->abqhd", rounded, values_cat, preferred_element_type=jnp.float32
    )
    attended_tiles = blended.astype(jnp.bfloat16)
    row_drift = jnp.sum(
        grad_tiles.astype(jnp.float32) * attended_tiles.astype(jnp.float32), axis=-1
    )
    drift_cols = jnp.swapaxes(row_drift, 2, 3)[..., None]
    products = jnp.einsum(
        "abqhd,abkhd->abhqk", grad_tiles, values_cat, preferred_element_type=jnp.float32
    )
    slopes = (weights * (products - drift_cols)).astype(jnp.bfloat16)
    query_sum = jnp.einsum(
        "abhqk,abkhd->abqhd", slopes, keys_cat, preferred_element_type=jnp.float32
    )
    attended = from_tiles(attended_tiles)
    query_grad = from_tiles(query_sum * scaling).astype(jnp.bfloat16)
    rim_shape = (tile_rows + 2, tile_cols + 2) + query_tiles.shape[2:]
    key_terms = jnp.einsum(
        "abhqk,abqhd->abkhd", slopes, query_tiles, preferred_element_type=jnp.float32
    )
    value_terms = jnp.einsum(
        "abhqk,abqhd->abkhd", rounded, grad_tiles, preferred_element_type=jnp.float32
    )
    key_part = jnp.zeros(rim_shape, jnp.float32)
    value_part = jnp.zeros(rim_shape, jnp.float32)
    for offset_index, (step_lat, step_lon) in enumerate(offsets):
        lower = offset_index * cells
        key_part = key_part.at[
            step_lat : step_lat + tile_rows, step_lon : step_lon + tile_cols
        ].add(key_terms[:, :, lower : lower + cells])
        value_part = value_part.at[
            step_lat : step_lat + tile_rows, step_lon : step_lon + tile_cols
        ].add(value_terms[:, :, lower : lower + cells])
    spread = jnp.concatenate([from_tiles(key_part * scaling), from_tiles(value_part)], axis=-1)
    from_west = from_behind(spread[:, :TILE].astype(jnp.bfloat16), "lon", -1).astype(jnp.float32)
    from_east = from_behind(spread[:, -TILE:].astype(jnp.bfloat16), "lon", 1).astype(jnp.float32)
    spread = spread.at[:, block_cols : block_cols + TILE].add(from_west)
    spread = spread.at[:, TILE : 2 * TILE].add(from_east)
    middle = spread[:, TILE : TILE + block_cols]
    from_north = shifted(middle[:TILE].astype(jnp.bfloat16), "lat", -1).astype(jnp.float32)
    from_south = shifted(middle[-TILE:].astype(jnp.bfloat16), "lat", 1).astype(jnp.float32)
    middle = middle.at[block_rows : block_rows + TILE].add(from_north)
    middle = middle.at[TILE : 2 * TILE].add(from_south)
    owned_cells = middle[TILE : TILE + block_rows]
    feature_count = key_field.shape[2]
    key_grad = owned_cells[:, :, :feature_count].astype(jnp.bfloat16)
    value_grad = owned_cells[:, :, feature_count:].astype(jnp.bfloat16)
    return (attended, query_grad, key_grad, value_grad)


def solution(mesh):
    return jax.shard_map(
        shards,
        mesh=mesh,
        in_specs=(
            P("lat", "lon", None),
            P("lat", "lon", None),
            P("lat", "lon", None),
            P("lat", "lon", None),
        ),
        out_specs=(
            P("lat", "lon", None),
            P("lat", "lon", None),
            P("lat", "lon", None),
            P("lat", "lon", None),
        ),
        check_vma=False,
    )
```

profile of v0, /device:TPU:54, one launch (start us, length us, event | category | flops | bytes accessed | tf_op | source)
XLA Modules:
  0.0 233.2 jit_solution(10359708613160853306)
XLA Ops:
  2.5 19.6 %collective-permute-start.1 = (bf16[8,16,1536]{2,1,0:T(8,128)(2,1)S(1)}, bf16[8,16,1536]{2,1,0:T(8,128)(2,1)S(1)}, u32[]{:S(2)}, u32[]{:S(2)}) collective-permute-start(bf16[8,16,1536]{2,1,0:T(8,128)(2,1)S(1)} %constant_dynamic-update-slice_fusion), channel_id=1, source_target_pairs={{32,0},{64,32},{96,64},{128,96},{160,128},{192,160},{224,192},{256... | collective-permute-start | bytes 1179656 | tf_op jit(solution)/shard_map/ppermute | solution.py:20
  25.3 11.3 %collective-permute-done.1 = bf16[8,16,1536]{2,1,0:T(8,128)(2,1)S(1)} collective-permute-done((bf16[8,16,1536]{2,1,0:T(8,128)(2,1)S(1)}, bf16[8,16,1536]{2,1,0:T(8,128)(2,1)S(1)}, u32[]{:S(2)}, u32[]{:S(2)}) %collective-permute-start.1) | collective-permute-done | bytes 393248 | tf_op jit(solution)/shard_map/ppermute | solution.py:20
  36.6 13.3 %collective-permute-done = bf16[8,16,1536]{2,1,0:T(8,128)(2,1)S(1)} collective-permute-done((bf16[8,16,1536]{2,1,0:T(8,128)(2,1)S(1)}, bf16[8,16,1536]{2,1,0:T(8,128)(2,1)S(1)}, u32[]{:S(2)}, u32[]{:S(2)}) %collective-permute-start) | collective-permute-done | bytes 393248 | tf_op jit(solution)/shard_map/ppermute | solution.py:18
  53.1 2.4 %collective-permute-start.2 = (bf16[24,8,1536]{2,1,0:T(8,128)(2,1)}, bf16[24,8,1536]{2,1,0:T(8,128)(2,1)}, u32[]{:S(2)}, u32[]{:S(2)}) collective-permute-start(bf16[24,8,1536]{2,1,0:T(8,128)(2,1)} %get-tuple-element.283), channel_id=1, source_target_pairs={{0,1},{1,2},{2,3},{3,4},{4,5},{5,6},{6,7},{7,8},{8,9},{9,10},{10,1... | collective-permute-start | bytes 1769480 | tf_op jit(solution)/shard_map/ppermute | solution.py:18
  61.6 3.0 %collective-permute-done.2 = bf16[24,8,1536]{2,1,0:T(8,128)(2,1)} collective-permute-done((bf16[24,8,1536]{2,1,0:T(8,128)(2,1)}, bf16[24,8,1536]{2,1,0:T(8,128)(2,1)}, u32[]{:S(2)}, u32[]{:S(2)}) %collective-permute-start.2) | collective-permute-done | bytes 589856 | tf_op jit(solution)/shard_map/ppermute | solution.py:18
  66.3 4.5 %reshape.1058 = bf16[3,8,4,8,24,64]{5,4,3,2,1,0:T(8,128)(2,1)} reshape(bf16[24,32,1536]{2,1,0:T(8,128)(2,1)S(1)} %pad_maximum_fusion.1) | data formatting | bytes 4718592 | tf_op jit(solution)/shard_map/reshape | solution.py:40
  70.8 3.5 %copy.60 = bf16[3,4,8,8,24,64]{5,4,3,2,1,0:T(8,128)(2,1)S(1)} copy(bf16[3,4,8,8,24,64]{5,4,3,1,2,0:T(8,128)(2,1)} %bitcast.117) | data formatting | bytes 4718592 | tf_op jit(solution)/shard_map/transpose | solution.py:43
  74.3 2.9 %fusion.53 = (bf16[1,2,64,24,64]{4,3,2,1,0:T(8,128)(2,1)S(1)}, bf16[1,2,64,24,64]{4,3,2,1,0:T(8,128)(2,1)S(1)}, bf16[1,2,64,24,64]{4,3,2,1,0:T(8,128)(2,1)S(1)},...) fusion(bf16[3,4,64,24,64]{4,3,2,1,0:T(8,128)(2,1)S(1)} %bitcast.116), kind=kLoop, calls=%fused_computation.94 | loop fusion | bytes 7077888 | tf_op jit(solution)/shard_map/slice | solution.py:58
  77.3 2.4 %copy.87 = bf16[1,2,64,24,64]{2,4,3,1,0:T(8,128)(2,1)} copy(bf16[1,2,64,24,64]{4,3,2,1,0:T(8,128)(2,1)} %get-tuple-element.278) | data formatting | bytes 786432
  79.7 2.5 %copy.88 = bf16[1,2,64,24,64]{2,4,3,1,0:T(8,128)(2,1)} copy(bf16[1,2,64,24,64]{4,3,2,1,0:T(8,128)(2,1)} %get-tuple-element.277) | data formatting | bytes 786432
  82.2 2.4 %copy.89 = bf16[1,2,64,24,64]{2,4,3,1,0:T(8,128)(2,1)} copy(bf16[1,2,64,24,64]{4,3,2,1,0:T(8,128)(2,1)} %get-tuple-element.276) | data formatting | bytes 786432
  84.6 2.4 %copy.90 = bf16[1,2,64,24,64]{2,4,3,1,0:T(8,128)(2,1)} copy(bf16[1,2,64,24,64]{4,3,2,1,0:T(8,128)(2,1)} %get-tuple-element.275) | data formatting | bytes 786432
  87.0 2.4 %copy.91 = bf16[1,2,64,24,64]{2,4,3,1,0:T(8,128)(2,1)} copy(bf16[1,2,64,24,64]{4,3,2,1,0:T(8,128)(2,1)} %get-tuple-element.274) | data formatting | bytes 786432
  89.4 2.4 %copy.92 = bf16[1,2,64,24,64]{2,4,3,1,0:T(8,128)(2,1)} copy(bf16[1,2,64,24,64]{4,3,2,1,0:T(8,128)(2,1)} %get-tuple-element.273) | data formatting | bytes 786432
  94.3 9.2 %concatenate.73 = bf16[1,2,576,24,64]{2,4,3,1,0:T(8,128)(2,1)} concatenate(bf16[1,2,64,24,64]{2,4,3,1,0:T(8,128)(2,1)} %copy.87, bf16[1,2,64,24,64]{2,4,3,1,0:T(8,128)(2,1)} %copy.88, bf16[1,2,64,24,64]{2,4,3,1,0:T(8,128)(2,1)} %copy.89, bf16[1,2,64,24,64]{2,4,3,1,0:T(8,128)(2,1)} %copy.90, bf16[1,2,64,24,64]{2,4,3,1,0:T(8,128)(2,1)} %copy.91, bf16[1,2,64,24,64]{2,4,3,1,0:T(8,128)(2,1)} %copy.92, ...), dimensions={2} | concatenate | bytes 7077888 | tf_op jit(solution)/shard_map/concatenate | solution.py:61
  103.5 2.4 %bitcast_reduce_fusion = (f32[2,12,64]{2,1,0:T(8,128)S(1)}, f32[2,12,576,64]{2,3,1,0:T(8,128)S(1)}) fusion(pred[576]{0:T(1024)(128)(4,1)S(1)} %reduce.54, bf16[1,2,576,24,64]{2,4,3,1,0:T(8,128)(2,1)} %concatenate.73, bf16[1,2,8,8,12,64]{5,4,3,1,2,0:T(8,128)(2,1)S(1)} %bitcast.120), kind=kOutput, calls=%fused_computation.7 | convolution fusion | flops 115898880 | bytes 5708352 | tf_op jit(solution)/shard_map/abqhd,abkhd->abhqk/dot_general | solution.py:92
  112.7 2.8 %scatter-add.81 = f32[3,4,64,12,64]{2,4,3,1,0:T(8,128)} pad(f32[1,2,64,12,64]{2,4,3,1,0:T(8,128)S(1)} %slice.991, f32[]{:T(128)} %constant.582.clone.1), padding=0_2x0_2x0_0x0_0x0_0 | pad | bytes 2752516 | tf_op jit(solution)/shard_map/scatter-add | solution.py:133
  115.5 2.6 %fusion.20 = (f32[3,4,64,12,64]{2,4,3,1,0:T(8,128)S(1)}, f32[3,4,64,12,64]{2,4,3,1,0:T(8,128)}) fusion(f32[3,4,64,12,64]{2,4,3,1,0:T(8,128)S(1)} %scatter-add.66, s32[]{:T(128)} %bitcast.26, s32[]{:T(128)} %bitcast.27, f32[1,2,64,12,64]{2,4,3,1,0:T(8,128)S(1)} %slice.976, f32[1,2,576,12,64]{2,4,3,1,0:T(8,128)S(1)} %convolution_bitcast_fusion.1, ...), kind=kLoop, calls=%fused_computation.40 | loop fusion | flops 196608 | bytes 4719616 | tf_op jit(solution)/shard_map/scatter-add | solution.py:130
  118.1 4.2 %fusion.18 = f32[3,4,64,12,64]{2,4,3,1,0:T(8,128)} fusion(f32[3,4,64,12,64]{2,4,3,1,0:T(8,128)} %get-tuple-element.296, s32[]{:T(128)} %bitcast.30, s32[]{:T(128)} %bitcast.31, f32[1,2,576,12,64]{2,4,3,1,0:T(8,128)S(1)} %convolution_bitcast_fusion, pred[]{:T(512)} %and_reduce_fusion), kind=kLoop, calls=%fused_computation.38 | loop fusion | flops 196608 | bytes 1967616 | tf_op jit(solution)/shard_map/scatter-add | solution.py:133
  135.7 6.4 %copy.83 = f32[3,4,64,12,64]{4,3,2,1,0:T(8,128)} copy(f32[3,4,64,12,64]{2,4,3,1,0:T(8,128)} %fusion.25) | data formatting | bytes 4718592 | tf_op jit(solution)/shard_map/scatter-add | solution.py:133
  142.2 5.5 %reshape.1074 = f32[3,4,8,8,768]{4,3,2,1,0:T(8,128)} reshape(f32[3,4,64,12,64]{4,3,2,1,0:T(8,128)} %copy.83) | data formatting | bytes 4718592 | tf_op jit(solution)/shard_map/reshape | solution.py:50
  150.5 4.2 %fusion.17 = f32[3,4,64,12,64]{2,4,3,1,0:T(8,128)} fusion(f32[3,4,64,12,64]{2,4,3,1,0:T(8,128)} %copy-done, s32[]{:T(128)} %bitcast.30, s32[]{:T(128)} %bitcast.31, f32[1,2,576,12,64]{2,4,3,1,0:T(8,128)S(1)} %copy-done.2, pred[]{:T(512)} %and_reduce_fusion), kind=kLoop, calls=%fused_computation.37 | loop fusion | flops 196608 | bytes 1967616 | tf_op jit(solution)/shard_map/scatter-add | solution.py:130
  154.6 2.4 %fusion.36 = f32[3,4,64,12,64]{2,4,3,1,0:T(8,128)} fusion(f32[3,4,64,12,64]{2,4,3,1,0:T(8,128)} %fusion.17, f32[1,2,576,12,64]{2,4,3,1,0:T(8,128)S(1)} %copy-done.2), kind=kLoop, calls=%fused_computation.69 | loop fusion | flops 98304 | bytes 1966080 | tf_op jit(solution)/shard_map/scatter-add | solution.py:130
  159.2 2.4 %fusion.34 = f32[3,4,64,12,64]{2,4,3,1,0:T(8,128)} fusion(f32[3,4,64,12,64]{2,4,3,1,0:T(8,128)} %fusion.35, f32[1,2,576,12,64]{2,4,3,1,0:T(8,128)S(1)} %copy-done.2), kind=kLoop, calls=%fused_computation.65 | loop fusion | flops 98304 | bytes 1966080 | tf_op jit(solution)/shard_map/scatter-add | solution.py:130
  168.1 5.5 %broadcast_multiply_fusion = f32[3,4,64,12,64]{2,4,3,1,0:T(8,128)} fusion(f32[3,4,64,12,64]{2,4,3,1,0:T(8,128)} %fusion.31), kind=kLoop, calls=%fused_computation.14 | loop fusion | flops 589824 | bytes 4718592 | tf_op jit(solution)/shard_map/mul | solution.py:134
  173.6 6.4 %copy.80 = f32[3,4,64,12,64]{4,3,2,1,0:T(8,128)} copy(f32[3,4,64,12,64]{2,4,3,1,0:T(8,128)} %broadcast_multiply_fusion) | data formatting | bytes 4718592 | tf_op jit(solution)/shard_map/mul | solution.py:134
  180.1 5.5 %reshape.1072 = f32[3,4,8,8,768]{4,3,2,1,0:T(8,128)} reshape(f32[3,4,64,12,64]{4,3,2,1,0:T(8,128)} %copy.80) | data formatting | bytes 4718592 | tf_op jit(solution)/shard_map/reshape | solution.py:50
  189.9 2.4 %collective-permute-start.5 = (bf16[24,8,1536]{2,1,0:T(8,128)(2,1)S(1)}, bf16[24,8,1536]{2,1,0:T(8,128)(2,1)S(1)}, u32[]{:S(2)}, u32[]{:S(2)}) collective-permute-start(bf16[24,8,1536]{2,1,0:T(8,128)(2,1)S(1)} %get-tuple-element.281), channel_id=1, source_target_pairs={{0,1},{1,2},{2,3},{3,4},{4,5},{5,6},{6,7},{7,8},{8,9},{9,10},{10,1... | collective-permute-start | bytes 1769480 | tf_op jit(solution)/shard_map/ppermute | solution.py:29
  192.9 4.4 %collective-permute-done.4 = bf16[24,8,1536]{2,1,0:T(8,128)(2,1)S(1)} collective-permute-done((bf16[24,8,1536]{2,1,0:T(8,128)(2,1)S(1)}, bf16[24,8,1536]{2,1,0:T(8,128)(2,1)S(1)}, u32[]{:S(2)}, u32[]{:S(2)}) %collective-permute-start.4) | collective-permute-done | bytes 589856 | tf_op jit(solution)/shard_map/ppermute | solution.py:29
  197.4 3.7 %collective-permute-done.5 = bf16[24,8,1536]{2,1,0:T(8,128)(2,1)S(1)} collective-permute-done((bf16[24,8,1536]{2,1,0:T(8,128)(2,1)S(1)}, bf16[24,8,1536]{2,1,0:T(8,128)(2,1)S(1)}, u32[]{:S(2)}, u32[]{:S(2)}) %collective-permute-start.5) | collective-permute-done | bytes 589856 | tf_op jit(solution)/shard_map/ppermute | solution.py:29
  206.0 9.9 %collective-permute-start.6 = (bf16[8,16,1536]{2,1,0:T(8,128)(2,1)S(1)}, bf16[8,16,1536]{2,1,0:T(8,128)(2,1)S(1)}, u32[]{:S(2)}, u32[]{:S(2)}) collective-permute-start(bf16[8,16,1536]{2,1,0:T(8,128)(2,1)S(1)} %get-tuple-element.279), channel_id=1, source_target_pairs={{32,0},{64,32},{96,64},{128,96},{160,128},{192,160},{224,192},{256... | collective-permute-start | bytes 1179656 | tf_op jit(solution)/shard_map/ppermute | solution.py:35
  219.0 12.2 %collective-permute-done.7 = bf16[8,16,1536]{2,1,0:T(8,128)(2,1)S(1)} collective-permute-done((bf16[8,16,1536]{2,1,0:T(8,128)(2,1)S(1)}, bf16[8,16,1536]{2,1,0:T(8,128)(2,1)S(1)}, u32[]{:S(2)}, u32[]{:S(2)}) %collective-permute-start.7) | collective-permute-done | bytes 393248 | tf_op jit(solution)/shard_map/ppermute | solution.py:35
  (95 shorter events, 64.9 us)
Async XLA Ops:
  2.5 34.1 %collective-permute-start.1 = (bf16[8,16,1536]{2,1,0:T(8,128)(2,1)S(1)}, bf16[8,16,1536]{2,1,0:T(8,128)(2,1)S(1)}, u32[]{:S(2)}, u32[]{:S(2)}) collective-permute-start(bf16[8,16,1536]{2,1,0:T(8,128)(2,1)S(1)} %constant_dynamic-update-slice_fusion), channel_id=1, source_target_pairs={{32,0},{64,32},{96,64},{128,96},{160,128},{192,160},{224,192},{256... | collective-permute-start | bytes 1179656 | tf_op jit(solution)/shard_map/ppermute | solution.py:20
  22.1 27.8 %collective-permute-start = (bf16[8,16,1536]{2,1,0:T(8,128)(2,1)S(1)}, bf16[8,16,1536]{2,1,0:T(8,128)(2,1)S(1)}, u32[]{:S(2)}, u32[]{:S(2)}) collective-permute-start(bf16[8,16,1536]{2,1,0:T(8,128)(2,1)S(1)} %constant_dynamic-update-slice_fusion), channel_id=1, source_target_pairs={{0,32},{32,64},{64,96},{96,128},{128,160},{160,192},{192,224},{224... | collective-permute-start | bytes 1179656 | tf_op jit(solution)/shard_map/ppermute | solution.py:18
  36.6 19.8 %copy-start.9 = (bf16[8,16,1536]{2,1,0:T(8,128)(2,1)}, bf16[8,16,1536]{2,1,0:T(8,128)(2,1)S(1)}, u32[]{:S(2)}) copy-start(bf16[8,16,1536]{2,1,0:T(8,128)(2,1)S(1)} %collective-permute-done.1) | copy-start | bytes 1179652
  49.9 6.6 %copy-start.10 = (bf16[8,16,1536]{2,1,0:T(8,128)(2,1)}, bf16[8,16,1536]{2,1,0:T(8,128)(2,1)S(1)}, u32[]{:S(2)}) copy-start(bf16[8,16,1536]{2,1,0:T(8,128)(2,1)S(1)} %collective-permute-done) | copy-start | bytes 1179652
  50.0 7.6 %copy-start.13 = (bf16[8,16,768]{2,1,0:T(8,128)(2,1)S(1)}, bf16[8,16,768]{2,1,0:T(8,128)(2,1)}, u32[]{:S(2)}) copy-start(bf16[8,16,768]{2,1,0:T(8,128)(2,1)} %param.48) | copy-start | bytes 589828
  50.1 9.3 %copy-start.14 = (s32[5]{0:T(128)S(1)}, s32[5]{0:T(128)}, u32[]{:S(2)}) copy-start(s32[5]{0:T(128)} %constant.585.clone.1) | copy-start | bytes 64
  51.2 9.6 %collective-permute-start.3 = (bf16[24,8,1536]{2,1,0:T(8,128)(2,1)}, bf16[24,8,1536]{2,1,0:T(8,128)(2,1)S(1)}, u32[]{:S(2)}, u32[]{:S(2)}) collective-permute-start(bf16[24,8,1536]{2,1,0:T(8,128)(2,1)} %get-tuple-element.284), channel_id=1, source_target_pairs={{1,0},{2,1},{3,2},{4,3},{5,4},{6,5},{7,6},{8,7},{9,8},{10,9},{11,1... | collective-permute-start | bytes 1769480 | tf_op jit(solution)/shard_map/ppermute | solution.py:20
  53.1 11.5 %collective-permute-start.2 = (bf16[24,8,1536]{2,1,0:T(8,128)(2,1)}, bf16[24,8,1536]{2,1,0:T(8,128)(2,1)}, u32[]{:S(2)}, u32[]{:S(2)}) collective-permute-start(bf16[24,8,1536]{2,1,0:T(8,128)(2,1)} %get-tuple-element.283), channel_id=1, source_target_pairs={{0,1},{1,2},{2,3},{3,4},{4,5},{5,6},{6,7},{7,8},{8,9},{9,10},{10,1... | collective-permute-start | bytes 1769480 | tf_op jit(solution)/shard_map/ppermute | solution.py:18
  60.8 0.8 copy-start.12
  103.4 3.5 %copy-start.4 = (bf16[1,2,576,24,64]{2,4,3,1,0:T(8,128)(2,1)S(1)}, bf16[1,2,576,24,64]{2,4,3,1,0:T(8,128)(2,1)}, u32[]{:S(2)}) copy-start(bf16[1,2,576,24,64]{2,4,3,1,0:T(8,128)(2,1)} %concatenate.73) | copy-start | bytes 10616836
  103.4 3.5 %copy-start.11 = (f32[1,2,64,12,64]{2,4,3,1,0:T(8,128)S(1)}, f32[1,2,64,12,64]{2,4,3,1,0:T(8,128)}, u32[]{:S(2)}) copy-start(f32[1,2,64,12,64]{2,4,3,1,0:T(8,128)} %copy.76) | copy-start | bytes 1179652
  107.0 1.2 copy-start.8
  110.7 1.4 copy-start.6
  111.4 4.1 %copy-start.1 = (f32[1,2,576,12,64]{2,4,3,1,0:T(8,128)}, f32[1,2,576,12,64]{2,4,3,1,0:T(8,128)S(1)}, u32[]{:S(2)}) copy-start(f32[1,2,576,12,64]{2,4,3,1,0:T(8,128)S(1)} %convolution_bitcast_fusion.1) | copy-start | bytes 10616836
  118.1 11.0 %copy-start = (f32[3,4,64,12,64]{2,4,3,1,0:T(8,128)}, f32[3,4,64,12,64]{2,4,3,1,0:T(8,128)S(1)}, u32[]{:S(2)}) copy-start(f32[3,4,64,12,64]{2,4,3,1,0:T(8,128)S(1)} %get-tuple-element.295) | copy-start | bytes 7077892
  147.6 2.8 %copy-start.2 = (f32[1,2,576,12,64]{2,4,3,1,0:T(8,128)S(1)}, f32[1,2,576,12,64]{2,4,3,1,0:T(8,128)}, u32[]{:S(2)}) copy-start(f32[1,2,576,12,64]{2,4,3,1,0:T(8,128)} %copy-done.1) | copy-start | bytes 10616836
  188.0 9.3 %collective-permute-start.4 = (bf16[24,8,1536]{2,1,0:T(8,128)(2,1)S(1)}, bf16[24,8,1536]{2,1,0:T(8,128)(2,1)S(1)}, u32[]{:S(2)}, u32[]{:S(2)}) collective-permute-start(bf16[24,8,1536]{2,1,0:T(8,128)(2,1)S(1)} %get-tuple-element.282), channel_id=1, source_target_pairs={{0,31},{1,0},{2,1},{3,2},{4,3},{5,4},{6,5},{7,6},{8,7},{9,8},{10,9... | collective-permute-start | bytes 1769480 | tf_op jit(solution)/shard_map/ppermute | solution.py:29
  189.9 11.2 %collective-permute-start.5 = (bf16[24,8,1536]{2,1,0:T(8,128)(2,1)S(1)}, bf16[24,8,1536]{2,1,0:T(8,128)(2,1)S(1)}, u32[]{:S(2)}, u32[]{:S(2)}) collective-permute-start(bf16[24,8,1536]{2,1,0:T(8,128)(2,1)S(1)} %get-tuple-element.281), channel_id=1, source_target_pairs={{0,1},{1,2},{2,3},{3,4},{4,5},{5,6},{6,7},{7,8},{8,9},{9,10},{10,1... | collective-permute-start | bytes 1769480 | tf_op jit(solution)/shard_map/ppermute | solution.py:29
  201.4 2.4 %copy-start.3 = (f32[24,32,1536]{2,1,0:T(8,128)}, f32[24,32,1536]{2,1,0:T(8,128)S(1)}, u32[]{:S(2)}) copy-start(f32[24,32,1536]{2,1,0:T(8,128)S(1)} %fusion.16) | copy-start | bytes 14155780
  201.4 14.5 %copy-start.5 = (bf16[1,2,576,24,64]{2,4,3,1,0:T(8,128)(2,1)S(1)}, bf16[1,2,576,24,64]{2,4,3,1,0:T(8,128)(2,1)}, u32[]{:S(2)}) copy-start(bf16[1,2,576,24,64]{2,4,3,1,0:T(8,128)(2,1)} %concatenate.73) | copy-start | bytes 10616836
  201.4 14.5 %copy-start.7 = (bf16[2,12,64,576]{3,2,1,0:T(8,128)(2,1)S(1)}, bf16[2,12,64,576]{3,2,1,0:T(8,128)(2,1)}, u32[]{:S(2)}) copy-start(bf16[2,12,64,576]{3,2,1,0:T(8,128)(2,1)} %copy-done.6) | copy-start | bytes 5308420
  203.8 27.4 %collective-permute-start.7 = (bf16[8,16,1536]{2,1,0:T(8,128)(2,1)S(1)}, bf16[8,16,1536]{2,1,0:T(8,128)(2,1)S(1)}, u32[]{:S(2)}, u32[]{:S(2)}) collective-permute-start(bf16[8,16,1536]{2,1,0:T(8,128)(2,1)S(1)} %get-tuple-element.280), channel_id=1, source_target_pairs={{0,32},{32,64},{64,96},{96,128},{128,160},{160,192},{192,224},{224... | collective-permute-start | bytes 1179656 | tf_op jit(solution)/shard_map/ppermute | solution.py:35
  206.0 25.2 %collective-permute-start.6 = (bf16[8,16,1536]{2,1,0:T(8,128)(2,1)S(1)}, bf16[8,16,1536]{2,1,0:T(8,128)(2,1)S(1)}, u32[]{:S(2)}, u32[]{:S(2)}) collective-permute-start(bf16[8,16,1536]{2,1,0:T(8,128)(2,1)S(1)} %get-tuple-element.279), channel_id=1, source_target_pairs={{32,0},{64,32},{96,64},{128,96},{160,128},{192,160},{224,192},{256... | collective-permute-start | bytes 1179656 | tf_op jit(solution)/shard_map/ppermute | solution.py:35
where the time goes:
time: 236 us; the launch traced here: 233 us
  local copies, waits for them, and re-layouts  82.8 us (35%)
  other arithmetic  50.9 us (22%)
  waiting for transfers between devices  48.5 us (21%)
  starting transfers between devices  42.2 us (18%)
  matrix products  7.6 us (3%)
    unnamed x40, local copies, waits for them, and re-layouts  22 us
    ppermute x2, starting transfers between devices, with_halo(): lax.ppermute(head, axis, [((i + 1) % count, i) for i in range(count)])  21.5 us
    scatter-add x8, other arithmetic, shards(): key_part = key_part.at[step_lat:step_lat + tile_rows, step_lon:step_lon +...  20.3 us
    scatter-add x7, other arithmetic, shards(): value_part = value_part.at[step_lat:step_lat + tile_rows, step_lon:step_l...  17.6 us
    ppermute x2, waiting for transfers between devices, with_halo(): lax.ppermute(tail, axis, [(i, (i + 1) % count) for i in range(count)])  16.3 us
    ppermute x2, waiting for transfers between devices, shifted(): lax.ppermute(value, axis, [(source, source + steps) for source in range(i...  12.2 us
    ppermute x2, starting transfers between devices, shifted(): lax.ppermute(value, axis, [(source, source + steps) for source in range(i...  12.1 us
    ppermute x2, waiting for transfers between devices, with_halo(): lax.ppermute(head, axis, [((i + 1) % count, i) for i in range(count)])  12 us
  transfers between devices with their start and end apart: 8, of which 7 were waited for; matrix products, arithmetic and copies ran while one was open for 4% of the time, Pallas kernels for 0%

commit v1 on v0

v1 whole, which is shorter than its diff:
```python
import jax
import jax.numpy as jnp
from jax import lax
from jax.experimental import pallas as pl
from jax.experimental.pallas import tpu as pltpu
from jax.sharding import PartitionSpec as P

HEAD_DIM = 64
TILE = 8
PAIR = 2 * HEAD_DIM
FAR = -1e30


def dot(a, b):
    return jnp.dot(a, b, preferred_element_type=jnp.float32)


def tile_order(x):
    width = x.shape[-1]
    return jnp.concatenate(
        [x[:, :TILE].reshape(TILE * TILE, width), x[:, TILE:].reshape(TILE * TILE, width)], axis=0
    )


def grid_order(x):
    width = x.shape[-1]
    half = TILE * TILE
    return jnp.concatenate(
        [x[:half].reshape(TILE, TILE, width), x[half:].reshape(TILE, TILE, width)], axis=1
    )


def attend_kernel(
    bias_ref, q_ref, g_ref, own_ref, north_ref, south_ref, west_ref, east_ref,
    att_ref, dq_ref, mid_ref, up_ref, down_ref, left_ref, right_ref,
):
    f32, bf16 = jnp.float32, jnp.bfloat16
    north_bias, south_bias = bias_ref[0], bias_ref[1]

    def keys(which):
        rows = [ref[which].reshape(PAIR, PAIR) for ref in (north_ref, own_ref, south_ref)]
        sides = [
            ref[which].astype(f32).reshape(3 * TILE * TILE, PAIR).astype(bf16)
            for ref in (west_ref, east_ref)
        ]
        return jnp.concatenate(rows + sides, axis=0)

    k_all, v_all = keys(0), keys(1)
    q_nat = tile_order(q_ref[...].astype(f32)) * (HEAD_DIM**-0.5)
    g_nat = tile_order(g_ref[...].astype(f32))
    q_turn, g_turn = q_nat.T, g_nat.T
    row = lax.broadcasted_iota(jnp.int32, (PAIR, PAIR), 0) < HEAD_DIM
    lane = lax.broadcasted_iota(jnp.int32, (PAIR, PAIR), 1) < HEAD_DIM

    def wide(x):
        return jnp.concatenate([jnp.where(row, x, 0.0), jnp.where(row, 0.0, x)], axis=1).astype(bf16)

    def tall(x):
        return jnp.concatenate([jnp.where(lane, x, 0.0), jnp.where(lane, 0.0, x)], axis=0).astype(bf16)

    core, side = 3 * PAIR, 3 * TILE * TILE
    in_west = (lax.broadcasted_iota(jnp.int32, (side, 2 * PAIR), 1) & HEAD_DIM) == 0

    def near(x):
        return jnp.concatenate(
            [x[:core], jnp.where(in_west, x[core : core + side], x[core + side :])], axis=0
        )

    def full(x):
        rest = x[core:]
        return jnp.concatenate(
            [x[:core], jnp.where(in_west, rest, 0.0), jnp.where(in_west, 0.0, rest)], axis=0
        ).astype(bf16)

    def diagonal(x):
        return jnp.concatenate([x[:HEAD_DIM, :PAIR], x[HEAD_DIM:, PAIR:]], axis=0)

    scores = near(dot(k_all, wide(q_turn)))
    half = TILE * TILE
    scores = jnp.concatenate(
        [
            scores[:PAIR] + north_bias,
            scores[PAIR : 2 * PAIR],
            scores[2 * PAIR : core] + south_bias,
            scores[core : core + half] + north_bias,
            scores[core + half : core + 2 * half],
            scores[core + 2 * half :] + south_bias,
        ],
        axis=0,
    )
    peak = jnp.max(scores, axis=0, keepdims=True)
    raised = jnp.exp(scores - peak)
    weights = raised * (1.0 / jnp.sum(raised, axis=0, keepdims=True))
    low = full(weights)
    att_turn = diagonal(dot(v_all.T, low)).astype(bf16).astype(f32)
    att_ref[...] = grid_order(att_turn.T).astype(bf16)
    product = g_turn * att_turn
    drift = jnp.concatenate(
        [
            jnp.sum(product[:HEAD_DIM], axis=0, keepdims=True),
            jnp.sum(product[HEAD_DIM:], axis=0, keepdims=True),
        ],
        axis=1,
    )
    slopes = full(weights * (near(dot(v_all, wide(g_turn))) - drift))
    dq_turn = diagonal(dot(k_all.T, slopes)) * (HEAD_DIM**-0.5)
    dq_ref[...] = grid_order(dq_turn.T).astype(bf16)
    for which, terms in ((0, dot(slopes, tall(q_nat))), (1, dot(low, tall(g_nat)))):
        up_ref[which] = terms[:PAIR].reshape(TILE, 2 * TILE, PAIR).astype(bf16)
        mid_ref[which] = terms[PAIR : 2 * PAIR].reshape(TILE, 2 * TILE, PAIR)
        down_ref[which] = terms[2 * PAIR : core].reshape(TILE, 2 * TILE, PAIR).astype(bf16)
        left_ref[which] = terms[core : core + side].reshape(3 * TILE, TILE, PAIR).astype(bf16)
        right_ref[which] = terms[core + side :].reshape(3 * TILE, TILE, PAIR).astype(bf16)


def attend(bias, q, g, own, north, south, west, east):
    width = q.shape[-1]
    grid3 = pl.BlockSpec((TILE, 2 * TILE, PAIR), lambda p: (0, 0, p))
    grid4 = pl.BlockSpec((2, TILE, 2 * TILE, PAIR), lambda p: (0, 0, 0, p))
    side4 = pl.BlockSpec((2, 3 * TILE, TILE, PAIR), lambda p: (0, 0, 0, p))
    shape = jax.ShapeDtypeStruct
    rows, cols = (2, TILE, 2 * TILE, width), (2, 3 * TILE, TILE, width)
    return pl.pallas_call(
        attend_kernel,
        grid=(width // PAIR,),
        in_specs=[pl.BlockSpec(memory_space=pltpu.SMEM), grid3, grid3, grid4, grid4, grid4, side4, side4],
        out_specs=[grid3, grid3, grid4, grid4, grid4, side4, side4],
        out_shape=[
            shape(q.shape, jnp.bfloat16),
            shape(q.shape, jnp.bfloat16),
            shape(rows, jnp.float32),
            shape(rows, jnp.bfloat16),
            shape(rows, jnp.bfloat16),
            shape(cols, jnp.bfloat16),
            shape(cols, jnp.bfloat16),
        ],
        compiler_params=pltpu.CompilerParams(vmem_limit_bytes=48 << 20),
        cost_estimate=pl.CostEstimate(flops=1 << 31, bytes_accessed=12 << 20, transcendentals=1 << 20),
        name="attend",
    )(bias, q, g, own, north, south, west, east)


def ring(value, steps):
    count = lax.axis_size("lon")
    return lax.ppermute(value, "lon", [(i, (i + steps) % count) for i in range(count)])


def line(value, steps):
    count = lax.axis_size("lat")
    first, last = max(0, -steps), min(count, count - steps)
    return lax.ppermute(value, "lat", [(i, i + steps) for i in range(first, last)])


def shards(query_field, key_field, value_field, out_cotangent):
    band = lax.axis_index("lat")
    bias = jnp.stack(
        [
            jnp.where(band == 0, FAR, 0.0),
            jnp.where(band == lax.axis_size("lat") - 1, FAR, 0.0),
        ]
    ).astype(jnp.float32)
    own = jnp.stack([key_field, value_field])
    north, south = line(own, 1), line(own, -1)
    first = jnp.concatenate([x[:, :, :TILE] for x in (north, own, south)], axis=1)
    second = jnp.concatenate([x[:, :, TILE:] for x in (north, own, south)], axis=1)
    west, east = ring(second, 1), ring(first, -1)
    att, dq, mid, up, down, left, right = attend(
        bias, query_field, out_cotangent, own, north, south, west, east
    )
    to_second, to_first = ring(left, -1), ring(right, 1)
    spread = jnp.concatenate([to_first, to_second], axis=2).astype(jnp.float32)
    up = (up.astype(jnp.float32) + spread[:, :TILE]).astype(jnp.bfloat16)
    down = (down.astype(jnp.float32) + spread[:, 2 * TILE :]).astype(jnp.bfloat16)
    from_south, from_north = line(up, -1), line(down, 1)
    total = (
        mid
        + spread[:, TILE : 2 * TILE]
        + from_south.astype(jnp.float32)
        + from_north.astype(jnp.float32)
    ).astype(jnp.bfloat16)
    return att, dq, total[0], total[1]


def solution(mesh):
    spec = P("lat", "lon", None)
    return jax.shard_map(
        shards, mesh=mesh, in_specs=(spec,) * 4, out_specs=(spec,) * 4, check_vma=False
    )
```

time: 236 us -> 119 us (0.50)
  the two profiles are of different devices: /device:TPU:54 before, /device:TPU:63 now
where the time goes in v1:
time: 119 us
  waiting for transfers between devices  64.1 us (54%)
  starting transfers between devices  38.5 us (32%)
  Pallas kernels  10.6 us (9%)
  other arithmetic  3.81 us (3%)
    ppermute x4, waiting for transfers between devices, line(): lax.ppermute(value, 'lat', [(i, i + steps) for i in range(first, last)])  38.1 us
    ppermute x4, starting transfers between devices, line(): lax.ppermute(value, 'lat', [(i, i + steps) for i in range(first, last)])  27.5 us
    ppermute x4, waiting for transfers between devices, ring(): lax.ppermute(value, 'lon', [(i, (i + steps) % count) for i in range(count)])  26 us
    ppermute x4, starting transfers between devices, ring(): lax.ppermute(value, 'lon', [(i, (i + steps) % count) for i in range(count)])  11 us
    pallas_call x1, Pallas kernels, attend(): pl.pallas_call(attend_kernel, grid=(width // PAIR,), in_specs=[pl.BlockSp...  10.6 us
  transfers between devices with their start and end apart: 8, of which 8 were waited for; matrix products, arithmetic and copies ran while one was open for 2% of the time, Pallas kernels for 0%

profile of v1, /device:TPU:63, one launch (start us, length us, event | category | flops | bytes accessed | tf_op | source)
XLA Modules:
  0.0 118.6 jit_solution(7841714447100750903)
XLA Ops:
  0.6 1.1 pad_maximum_fusion.2.own_ref
  1.7 0.0 copy-start
  1.7 0.0 copy-start.1
  1.7 20.3 %collective-permute-start.1 = (bf16[2,8,16,768]{3,2,1,0:T(8,128)(2,1)S(1)}, bf16[2,8,16,768]{3,2,1,0:T(8,128)(2,1)S(1)}, u32[]{:S(2)}, u32[]{:S(2)}) collective-permute-start(bf16[2,8,16,768]{3,2,1,0:T(8,128)(2,1)S(1)} %pad_maximum_fusion.2.own_ref), channel_id=1, source_target_pairs={{32,0},{64,32},{96,64},{128,96},{160,128},{192,160},{224,192},{256... | collective-permute-start | bytes 1179656 | tf_op jit(solution)/shard_map/ppermute | solution.py:151
  22.0 1.9 %collective-permute-start = (bf16[2,8,16,768]{3,2,1,0:T(8,128)(2,1)S(1)}, bf16[2,8,16,768]{3,2,1,0:T(8,128)(2,1)S(1)}, u32[]{:S(2)}, u32[]{:S(2)}) collective-permute-start(bf16[2,8,16,768]{3,2,1,0:T(8,128)(2,1)S(1)} %pad_maximum_fusion.2.own_ref), channel_id=1, source_target_pairs={{0,32},{32,64},{64,96},{96,128},{128,160},{160,192},{192,224},{224... | collective-permute-start | bytes 1179656 | tf_op jit(solution)/shard_map/ppermute | solution.py:151
  24.0 1.1 fusion.6
  25.1 8.0 %collective-permute-done.1.south_ref = bf16[2,8,16,768]{3,2,1,0:T(8,128)(2,1)S(1)} collective-permute-done((bf16[2,8,16,768]{3,2,1,0:T(8,128)(2,1)S(1)}, bf16[2,8,16,768]{3,2,1,0:T(8,128)(2,1)S(1)}, u32[]{:S(2)}, u32[]{:S(2)}) %collective-permute-start.1) | collective-permute-done | bytes 393248 | tf_op jit(solution)/shard_map/ppermute | solution.py:151
  33.1 13.7 %collective-permute-done.north_ref = bf16[2,8,16,768]{3,2,1,0:T(8,128)(2,1)S(1)} collective-permute-done((bf16[2,8,16,768]{3,2,1,0:T(8,128)(2,1)S(1)}, bf16[2,8,16,768]{3,2,1,0:T(8,128)(2,1)S(1)}, u32[]{:S(2)}, u32[]{:S(2)}) %collective-permute-start) | collective-permute-done | bytes 393248 | tf_op jit(solution)/shard_map/ppermute | solution.py:151
  46.8 0.1 pad_maximum_fusion
  46.9 4.7 %collective-permute-start.2 = (bf16[2,24,8,768]{3,2,1,0:T(8,128)(2,1)S(1)}, bf16[2,24,8,768]{3,2,1,0:T(8,128)(2,1)S(1)}, u32[]{:S(2)}, u32[]{:S(2)}) collective-permute-start(bf16[2,24,8,768]{3,2,1,0:T(8,128)(2,1)S(1)} %pad_maximum_fusion), channel_id=1, source_target_pairs={{0,1},{1,2},{2,3},{3,4},{4,5},{5,6},{6,7},{7,8},{8,9},{9,10},{10,1... | collective-permute-start | bytes 1769480 | tf_op jit(solution)/shard_map/ppermute | solution.py:145
  51.6 0.9 pad_maximum_fusion.1
  52.5 1.9 %collective-permute-start.3 = (bf16[2,24,8,768]{3,2,1,0:T(8,128)(2,1)}, bf16[2,24,8,768]{3,2,1,0:T(8,128)(2,1)S(1)}, u32[]{:S(2)}, u32[]{:S(2)}) collective-permute-start(bf16[2,24,8,768]{3,2,1,0:T(8,128)(2,1)} %pad_maximum_fusion.1), channel_id=1, source_target_pairs={{0,31},{1,0},{2,1},{3,2},{4,3},{5,4},{6,5},{7,6},{8,7},{9,8},{10,9... | collective-permute-start | bytes 1769480 | tf_op jit(solution)/shard_map/ppermute | solution.py:145
  54.4 0.1 pad_maximum_fusion.3.bias_ref
  54.5 3.9 %collective-permute-done.2.west_ref = bf16[2,24,8,768]{3,2,1,0:T(8,128)(2,1)S(1)} collective-permute-done((bf16[2,24,8,768]{3,2,1,0:T(8,128)(2,1)S(1)}, bf16[2,24,8,768]{3,2,1,0:T(8,128)(2,1)S(1)}, u32[]{:S(2)}, u32[]{:S(2)}) %collective-permute-start.2) | collective-permute-done | bytes 589856 | tf_op jit(solution)/shard_map/ppermute | solution.py:145
  58.4 9.4 %collective-permute-done.3.east_ref = bf16[2,24,8,768]{3,2,1,0:T(8,128)(2,1)S(1)} collective-permute-done((bf16[2,24,8,768]{3,2,1,0:T(8,128)(2,1)}, bf16[2,24,8,768]{3,2,1,0:T(8,128)(2,1)S(1)}, u32[]{:S(2)}, u32[]{:S(2)}) %collective-permute-start.3) | collective-permute-done | bytes 589856 | tf_op jit(solution)/shard_map/ppermute | solution.py:145
  67.8 0.0 copy-done
  67.8 0.0 copy-done.1
  67.8 10.6 %attend.1 = (bf16[8,16,768]{2,1,0:T(8,128)(2,1)}, bf16[8,16,768]{2,1,0:T(8,128)(2,1)}, f32[2,8,16,768]{3,2,1,0:T(8,128)S(1)}, bf16[2,8,16,768]{3,2,1,0:T(8,128)(...) custom-call(f32[2]{0:T(128)S(1)} %pad_maximum_fusion.3.bias_ref, ...), custom_call_target="tpu_custom_call" | custom-call | flops 2147483648 | bytes 12582912 | tf_op jit(solution)/shard_map/attend/pallas_call | solution.py:123
  78.4 1.9 %collective-permute-start.4 = (bf16[2,24,8,768]{3,2,1,0:T(8,128)(2,1)S(1)}, bf16[2,24,8,768]{3,2,1,0:T(8,128)(2,1)S(1)}, u32[]{:S(2)}, u32[]{:S(2)}) collective-permute-start(bf16[2,24,8,768]{3,2,1,0:T(8,128)(2,1)S(1)} %get-tuple-element.14), channel_id=1, source_target_pairs={{0,1},{1,2},{2,3},{3,4},{4,5},{5,6},{6,7},{7,8},{8,9},{9,10},{10,1... | collective-permute-start | bytes 1769480 | tf_op jit(solution)/shard_map/ppermute | solution.py:145
  80.3 2.4 %collective-permute-start.5 = (bf16[2,24,8,768]{3,2,1,0:T(8,128)(2,1)S(1)}, bf16[2,24,8,768]{3,2,1,0:T(8,128)(2,1)S(1)}, u32[]{:S(2)}, u32[]{:S(2)}) collective-permute-start(bf16[2,24,8,768]{3,2,1,0:T(8,128)(2,1)S(1)} %get-tuple-element.15), channel_id=1, source_target_pairs={{0,31},{1,0},{2,1},{3,2},{4,3},{5,4},{6,5},{7,6},{8,7},{9,8},{10,9... | collective-permute-start | bytes 1769480 | tf_op jit(solution)/shard_map/ppermute | solution.py:145
  82.7 4.4 %collective-permute-done.4 = bf16[2,24,8,768]{3,2,1,0:T(8,128)(2,1)S(1)} collective-permute-done((bf16[2,24,8,768]{3,2,1,0:T(8,128)(2,1)S(1)}, bf16[2,24,8,768]{3,2,1,0:T(8,128)(2,1)S(1)}, u32[]{:S(2)}, u32[]{:S(2)}) %collective-permute-start.4) | collective-permute-done | bytes 589856 | tf_op jit(solution)/shard_map/ppermute | solution.py:145
  87.1 8.3 %collective-permute-done.5 = bf16[2,24,8,768]{3,2,1,0:T(8,128)(2,1)S(1)} collective-permute-done((bf16[2,24,8,768]{3,2,1,0:T(8,128)(2,1)S(1)}, bf16[2,24,8,768]{3,2,1,0:T(8,128)(2,1)S(1)}, u32[]{:S(2)}, u32[]{:S(2)}) %collective-permute-start.5) | collective-permute-done | bytes 589856 | tf_op jit(solution)/shard_map/ppermute | solution.py:145
  95.4 0.2 maximum_convert_fusion
  95.6 0.2 fusion.1
  95.9 1.9 %collective-permute-start.6 = (bf16[2,8,16,768]{3,2,1,0:T(8,128)(2,1)S(1)}, bf16[2,8,16,768]{3,2,1,0:T(8,128)(2,1)S(1)}, u32[]{:S(2)}, u32[]{:S(2)}) collective-permute-start(bf16[2,8,16,768]{3,2,1,0:T(8,128)(2,1)S(1)} %get-tuple-element.18), channel_id=1, source_target_pairs={{32,0},{64,32},{96,64},{128,96},{160,128},{192,160},{224,192},{256... | collective-permute-start | bytes 1179656 | tf_op jit(solution)/shard_map/ppermute | solution.py:151
  97.8 3.4 %collective-permute-start.7 = (bf16[2,8,16,768]{3,2,1,0:T(8,128)(2,1)S(1)}, bf16[2,8,16,768]{3,2,1,0:T(8,128)(2,1)S(1)}, u32[]{:S(2)}, u32[]{:S(2)}) collective-permute-start(bf16[2,8,16,768]{3,2,1,0:T(8,128)(2,1)S(1)} %get-tuple-element.19), channel_id=1, source_target_pairs={{0,32},{32,64},{64,96},{96,128},{128,160},{160,192},{192,224},{224... | collective-permute-start | bytes 1179656 | tf_op jit(solution)/shard_map/ppermute | solution.py:151
  101.2 4.8 %collective-permute-done.6 = bf16[2,8,16,768]{3,2,1,0:T(8,128)(2,1)S(1)} collective-permute-done((bf16[2,8,16,768]{3,2,1,0:T(8,128)(2,1)S(1)}, bf16[2,8,16,768]{3,2,1,0:T(8,128)(2,1)S(1)}, u32[]{:S(2)}, u32[]{:S(2)}) %collective-permute-start.6) | collective-permute-done | bytes 393248 | tf_op jit(solution)/shard_map/ppermute | solution.py:151
  106.0 11.6 %collective-permute-done.7 = bf16[2,8,16,768]{3,2,1,0:T(8,128)(2,1)S(1)} collective-permute-done((bf16[2,8,16,768]{3,2,1,0:T(8,128)(2,1)S(1)}, bf16[2,8,16,768]{3,2,1,0:T(8,128)(2,1)S(1)}, u32[]{:S(2)}, u32[]{:S(2)}) %collective-permute-start.7) | collective-permute-done | bytes 393248 | tf_op jit(solution)/shard_map/ppermute | solution.py:151
  117.6 0.3 fusion.4
  117.8 0.8 slice_bitcast_fusion
  (2 shorter events, 0.1 us)
Async XLA Ops:
  1.7 66.1 %copy-start = (bf16[8,16,768]{2,1,0:T(8,128)(2,1)S(1)}, bf16[8,16,768]{2,1,0:T(8,128)(2,1)}, u32[]{:S(2)}) copy-start(bf16[8,16,768]{2,1,0:T(8,128)(2,1)} %q_ref.1) | copy-start | bytes 589828
  1.7 66.1 %copy-start.1 = (bf16[8,16,768]{2,1,0:T(8,128)(2,1)S(1)}, bf16[8,16,768]{2,1,0:T(8,128)(2,1)}, u32[]{:S(2)}) copy-start(bf16[8,16,768]{2,1,0:T(8,128)(2,1)} %g_ref.1) | copy-start | bytes 589828
  1.7 31.3 %collective-permute-start.1 = (bf16[2,8,16,768]{3,2,1,0:T(8,128)(2,1)S(1)}, bf16[2,8,16,768]{3,2,1,0:T(8,128)(2,1)S(1)}, u32[]{:S(2)}, u32[]{:S(2)}) collective-permute-start(bf16[2,8,16,768]{3,2,1,0:T(8,128)(2,1)S(1)} %pad_maximum_fusion.2.own_ref), channel_id=1, source_target_pairs={{32,0},{64,32},{96,64},{128,96},{160,128},{192,160},{224,192},{256... | collective-permute-start | bytes 1179656 | tf_op jit(solution)/shard_map/ppermute | solution.py:151
  22.0 24.7 %collective-permute-start = (bf16[2,8,16,768]{3,2,1,0:T(8,128)(2,1)S(1)}, bf16[2,8,16,768]{3,2,1,0:T(8,128)(2,1)S(1)}, u32[]{:S(2)}, u32[]{:S(2)}) collective-permute-start(bf16[2,8,16,768]{3,2,1,0:T(8,128)(2,1)S(1)} %pad_maximum_fusion.2.own_ref), channel_id=1, source_target_pairs={{0,32},{32,64},{64,96},{96,128},{128,160},{160,192},{192,224},{224... | collective-permute-start | bytes 1179656 | tf_op jit(solution)/shard_map/ppermute | solution.py:151
  46.9 11.5 %collective-permute-start.2 = (bf16[2,24,8,768]{3,2,1,0:T(8,128)(2,1)S(1)}, bf16[2,24,8,768]{3,2,1,0:T(8,128)(2,1)S(1)}, u32[]{:S(2)}, u32[]{:S(2)}) collective-permute-start(bf16[2,24,8,768]{3,2,1,0:T(8,128)(2,1)S(1)} %pad_maximum_fusion), channel_id=1, source_target_pairs={{0,1},{1,2},{2,3},{3,4},{4,5},{5,6},{6,7},{7,8},{8,9},{9,10},{10,1... | collective-permute-start | bytes 1769480 | tf_op jit(solution)/shard_map/ppermute | solution.py:145
  52.5 15.3 %collective-permute-start.3 = (bf16[2,24,8,768]{3,2,1,0:T(8,128)(2,1)}, bf16[2,24,8,768]{3,2,1,0:T(8,128)(2,1)S(1)}, u32[]{:S(2)}, u32[]{:S(2)}) collective-permute-start(bf16[2,24,8,768]{3,2,1,0:T(8,128)(2,1)} %pad_maximum_fusion.1), channel_id=1, source_target_pairs={{0,31},{1,0},{2,1},{3,2},{4,3},{5,4},{6,5},{7,6},{8,7},{9,8},{10,9... | collective-permute-start | bytes 1769480 | tf_op jit(solution)/shard_map/ppermute | solution.py:145
  78.4 8.7 %collective-permute-start.4 = (bf16[2,24,8,768]{3,2,1,0:T(8,128)(2,1)S(1)}, bf16[2,24,8,768]{3,2,1,0:T(8,128)(2,1)S(1)}, u32[]{:S(2)}, u32[]{:S(2)}) collective-permute-start(bf16[2,24,8,768]{3,2,1,0:T(8,128)(2,1)S(1)} %get-tuple-element.14), channel_id=1, source_target_pairs={{0,1},{1,2},{2,3},{3,4},{4,5},{5,6},{6,7},{7,8},{8,9},{9,10},{10,1... | collective-permute-start | bytes 1769480 | tf_op jit(solution)/shard_map/ppermute | solution.py:145
  80.3 15.1 %collective-permute-start.5 = (bf16[2,24,8,768]{3,2,1,0:T(8,128)(2,1)S(1)}, bf16[2,24,8,768]{3,2,1,0:T(8,128)(2,1)S(1)}, u32[]{:S(2)}, u32[]{:S(2)}) collective-permute-start(bf16[2,24,8,768]{3,2,1,0:T(8,128)(2,1)S(1)} %get-tuple-element.15), channel_id=1, source_target_pairs={{0,31},{1,0},{2,1},{3,2},{4,3},{5,4},{6,5},{7,6},{8,7},{9,8},{10,9... | collective-permute-start | bytes 1769480 | tf_op jit(solution)/shard_map/ppermute | solution.py:145
  95.9 10.1 %collective-permute-start.6 = (bf16[2,8,16,768]{3,2,1,0:T(8,128)(2,1)S(1)}, bf16[2,8,16,768]{3,2,1,0:T(8,128)(2,1)S(1)}, u32[]{:S(2)}, u32[]{:S(2)}) collective-permute-start(bf16[2,8,16,768]{3,2,1,0:T(8,128)(2,1)S(1)} %get-tuple-element.18), channel_id=1, source_target_pairs={{32,0},{64,32},{96,64},{128,96},{160,128},{192,160},{224,192},{256... | collective-permute-start | bytes 1179656 | tf_op jit(solution)/shard_map/ppermute | solution.py:151
  97.8 19.8 %collective-permute-start.7 = (bf16[2,8,16,768]{3,2,1,0:T(8,128)(2,1)S(1)}, bf16[2,8,16,768]{3,2,1,0:T(8,128)(2,1)S(1)}, u32[]{:S(2)}, u32[]{:S(2)}) collective-permute-start(bf16[2,8,16,768]{3,2,1,0:T(8,128)(2,1)S(1)} %get-tuple-element.19), channel_id=1, source_target_pairs={{0,32},{32,64},{64,96},{96,128},{128,160},{160,192},{192,224},{224... | collective-permute-start | bytes 1179656 | tf_op jit(solution)/shard_map/ppermute | solution.py:151
